TPU v7x, 256 devices: a whole 4x4x8 slice. The times are simulated.
256 devices in a mesh: lat: 8 (over x, core), lon: 32 (over z, y).
Axes of the slice: x: 4, y: 4, z: 8, core: 2. Of those that a mesh axis runs over, the one named last changes fastest.
Arguments:
- features: bfloat16 [256, 512, 768], P('lat', 'lon'), may hold values from -6 to 6
- cotangent: bfloat16 [256, 512, 768], P('lat', 'lon'), may hold values from -6 to 6
- weight_first: bfloat16 [2, 8, 96, 96], replicated, may hold values from -1 to 1
- weight_second: bfloat16 [2, 8, 96, 96], replicated, may hold values from -1 to 1
Outputs:
- mixed_field: bfloat16 [256, 512, 768], P('lat', 'lon')
- feature_grad: bfloat16 [256, 512, 768], P('lat', 'lon')
- grad_first: float32 [2, 8, 96, 96], replicated
- grad_second: float32 [2, 8, 96, 96], replicated
All inputs are finite; a program needn't handle non-finite values.
Results may differ from a plain program's by a relative error of at most 0.012.
The roundings to bfloat16 on the way count: a program that leaves them out, or rounds other values in their place, can miss the bound.
Values may be sent and summed in bfloat16 or wider, within the bound.
A program may use at most 64 MiB of HBM per device.

v0:
```python
import math
import jax
import jax.numpy as jnp
from jax import lax
from jax.sharding import PartitionSpec as P

NB = 8
BS = 96
KWD = 1
shrink_level = 0.01
gelu_coeff = 0.7978845608028654


def wave_table(first, second, length):
    product = first[:, None] * second[None, :] % length
    angle = 2.0 * math.pi / length * product.astype(jnp.float32)
    return (jnp.cos(angle) / math.sqrt(length), jnp.sin(angle) / math.sqrt(length))


def batch_product(left, weights):
    return jnp.einsum("mbi,bio->mbo", left, weights, preferred_element_type=jnp.float32)


def batch_back(left, weights):
    return jnp.einsum("mbo,bio->mbi", left, weights, preferred_element_type=jnp.float32)


def batch_outer(left, right):
    return jnp.einsum("mbi,mbo->bio", left, right, preferred_element_type=jnp.float32)


def gelu_parts(values):
    squared = values * values
    tangent = jnp.tanh(gelu_coeff * (values + 0.044715 * squared * values))
    result = 0.5 * values * (1.0 + tangent)
    slope = 0.5 * (1.0 + tangent) + 0.5 * values * (1.0 - tangent * tangent) * gelu_coeff * (
        1.0 + 3.0 * 0.044715 * squared
    )
    return (result, slope)


def shrink_parts(values):
    ratio = jnp.tanh(values / shrink_level)
    return (values - shrink_level * ratio, ratio * ratio)


def spectral_block(real_in, imag_in, real_cot, imag_cot, mode_weight, weight_first, weight_second):
    first_re, first_im = (weight_first[0], weight_first[1])
    second_re, second_im = (weight_second[0], weight_second[1])
    pre_real = batch_product(real_in, first_re) - batch_product(imag_in, first_im)
    pre_imag = batch_product(real_in, first_im) + batch_product(imag_in, first_re)
    act_real, slope_real = gelu_parts(pre_real)
    act_imag, slope_imag = gelu_parts(pre_imag)
    hidden_real = act_real.astype(jnp.bfloat16)
    hidden_imag = act_imag.astype(jnp.bfloat16)
    post_real = batch_product(hidden_real, second_re) - batch_product(hidden_imag, second_im)
    post_imag = batch_product(hidden_real, second_im) + batch_product(hidden_imag, second_re)
    shr_real, pass_real = shrink_parts(post_real)
    shr_imag, pass_imag = shrink_parts(post_imag)
    out_real = shr_real.astype(jnp.bfloat16)
    out_imag = shr_imag.astype(jnp.bfloat16)
    grad_post_real = (mode_weight * real_cot.astype(jnp.float32) * pass_real).astype(jnp.bfloat16)
    grad_post_imag = (mode_weight * imag_cot.astype(jnp.float32) * pass_imag).astype(jnp.bfloat16)
    grad_hid_real = batch_back(grad_post_real, second_re) + batch_back(grad_post_imag, second_im)
    grad_hid_imag = batch_back(grad_post_imag, second_re) - batch_back(grad_post_real, second_im)
    grad_pre_real = (grad_hid_real * slope_real).astype(jnp.bfloat16)
    grad_pre_imag = (grad_hid_imag * slope_imag).astype(jnp.bfloat16)
    back_real = (batch_back(grad_pre_real, first_re) + batch_back(grad_pre_imag, first_im)).astype(
        jnp.bfloat16
    )
    back_imag = (batch_back(grad_pre_imag, first_re) - batch_back(grad_pre_real, first_im)).astype(
        jnp.bfloat16
    )
    grad_second = jnp.stack(
        [
            batch_outer(hidden_real, grad_post_real) + batch_outer(hidden_imag, grad_post_imag),
            batch_outer(hidden_real, grad_post_imag) - batch_outer(hidden_imag, grad_post_real),
        ]
    )
    grad_first = jnp.stack(
        [
            batch_outer(real_in, grad_pre_real) + batch_outer(imag_in, grad_pre_imag),
            batch_outer(real_in, grad_pre_imag) - batch_outer(imag_in, grad_pre_real),
        ]
    )
    return (out_real, out_imag, back_real, back_imag, grad_first, grad_second)


def lon_transpose(source, split_dim, concat_dim):
    return lax.all_to_all(source, "lon", split_axis=split_dim, concat_axis=concat_dim, tiled=True)


def shards(features, cotangent, weight_first, weight_second):
    lat_count = lax.axis_size("lat")
    lon_count = lax.axis_size("lon")
    lat_index = lax.axis_index("lat")
    lon_index = lax.axis_index("lon")
    band_rows, band_cols, channels = features.shape
    rows_total = band_rows * lat_count
    cols_total = band_cols * lon_count
    rows_each = band_rows // lon_count
    kept_total = KWD * lat_count * lon_count
    stacked = jnp.stack([features, cotangent])
    full_rows = lon_transpose(stacked, 1, 2)
    lon_cos, lon_sin = wave_table(
        jnp.arange(kept_total, dtype=jnp.int32), jnp.arange(cols_total, dtype=jnp.int32), cols_total
    )
    lon_coeffs = jnp.concatenate([lon_cos, lon_sin]).astype(jnp.bfloat16)
    product = jnp.einsum(
        "aw,rwc->rac",
        lon_coeffs,
        full_rows.reshape(2 * rows_each, cols_total, channels),
        preferred_element_type=jnp.float32,
    )
    spectral_rows = jnp.stack([product[:, :kept_total], -product[:, kept_total:]], axis=1).astype(
        jnp.bfloat16
    )
    spectral_rows = spectral_rows.reshape(2, rows_each, 2, kept_total, channels)
    gathered = lax.all_to_all(
        lax.all_to_all(spectral_rows, "lat", split_axis=3, concat_axis=1, tiled=True),
        "lon",
        split_axis=3,
        concat_axis=1,
        tiled=True,
    )
    position = jnp.arange(rows_total, dtype=jnp.int32)
    row_of = (
        position // rows_each % lat_count * band_rows
        + position // (lat_count * rows_each) * rows_each
        + position % rows_each
    )
    lat_cos, lat_sin = wave_table(jnp.arange(rows_total, dtype=jnp.int32), row_of, rows_total)
    lat_coeffs = jnp.concatenate([lat_cos, lat_sin]).astype(jnp.bfloat16)
    product = jnp.einsum(
        "ah,shrc->sarc",
        lat_coeffs,
        gathered.reshape(2, rows_total, 2, KWD * channels),
        preferred_element_type=jnp.float32,
    )
    upper = product[:, :rows_total]
    lower = product[:, rows_total:]
    spec_real = (upper[:, :, 0] + lower[:, :, 1]).astype(jnp.bfloat16)
    spec_imag = (upper[:, :, 1] - lower[:, :, 0]).astype(jnp.bfloat16)
    modes = rows_total * KWD
    held_kw = (lat_index * lon_count + lon_index) * KWD + jnp.arange(KWD, dtype=jnp.int32)
    mode_weight = jnp.broadcast_to(
        jnp.where(held_kw == 0, 1.0, 2.0).astype(jnp.float32)[None, :], (rows_total, KWD)
    ).reshape(modes, 1, 1)
    results = spectral_block(
        spec_real[0].reshape(modes, NB, BS),
        spec_imag[0].reshape(modes, NB, BS),
        spec_real[1].reshape(modes, NB, BS),
        spec_imag[1].reshape(modes, NB, BS),
        mode_weight,
        weight_first,
        weight_second,
    )
    out_real, out_imag, back_real, back_imag, grad_first, grad_second = results
    spec_out = jnp.stack(
        [jnp.stack([out_real, out_imag]), jnp.stack([back_real, back_imag])]
    ).reshape(2, 2, rows_total, KWD * channels)
    nat_cos, nat_sin = wave_table(
        jnp.arange(rows_total, dtype=jnp.int32), jnp.arange(rows_total, dtype=jnp.int32), rows_total
    )
    nat_coeffs = jnp.concatenate([nat_cos, nat_sin]).astype(jnp.bfloat16)
    product = jnp.einsum("ak,sqkc->saqc", nat_coeffs, spec_out, preferred_element_type=jnp.float32)
    upper = product[:, :rows_total]
    lower = product[:, rows_total:]
    inverse_rows = jnp.stack(
        [upper[:, :, 0] - lower[:, :, 1], lower[:, :, 0] + upper[:, :, 1]], axis=2
    ).astype(jnp.bfloat16)
    inverse_rows = inverse_rows.reshape(2, rows_total, 2, KWD, channels)
    returned = lax.all_to_all(
        lax.all_to_all(inverse_rows, "lat", split_axis=1, concat_axis=3, tiled=True),
        "lon",
        split_axis=1,
        concat_axis=3,
        tiled=True,
    )
    slot_index = jnp.arange(kept_total, dtype=jnp.int32)
    kw_of = (
        slot_index // KWD % lat_count * lon_count + slot_index // (lat_count * KWD)
    ) * KWD + slot_index % KWD
    inv_cos, inv_sin = wave_table(kw_of, jnp.arange(cols_total, dtype=jnp.int32), cols_total)
    plain = jnp.concatenate([inv_cos, -inv_sin]).astype(jnp.bfloat16)
    doubled = jnp.where(kw_of == 0, 1.0, 2.0).astype(jnp.float32)
    scaled = (plain.astype(jnp.float32) * jnp.concatenate([doubled, doubled])[:, None]).astype(
        jnp.bfloat16
    )
    returned_flat = returned.reshape(2, rows_each, 2 * kept_total, channels)
    filtered = jnp.einsum(
        "aw,rac->rwc", scaled, returned_flat[0], preferred_element_type=jnp.float32
    ).astype(jnp.bfloat16)
    backward = jnp.einsum(
        "aw,rac->rwc", plain, returned_flat[1], preferred_element_type=jnp.float32
    ).astype(jnp.bfloat16)
    spatial = lon_transpose(jnp.stack([filtered, backward]), 2, 1)
    mixed_field = (features.astype(jnp.float32) + spatial[0].astype(jnp.float32)).astype(
        jnp.bfloat16
    )
    feature_grad = (cotangent.astype(jnp.float32) + spatial[1].astype(jnp.float32)).astype(
        jnp.bfloat16
    )
    summed = lax.psum((grad_first, grad_second), ("lat", "lon"))
    factor = 1.0 / math.sqrt(rows_total * kept_total)
    return (mixed_field, feature_grad, summed[0] * factor, summed[1] * factor)


def solution(mesh):
    in_specs = (P("lat", "lon", None), P("lat", "lon", None), P(), P())
    out_specs = (P("lat", "lon", None), P("lat", "lon", None), P(), P())
    return jax.shard_map(shards, mesh=mesh, in_specs=in_specs, out_specs=out_specs, check_vma=False)
```

profile of v0, /device:TPU:2, one launch (start us, length us, event | category | flops | bytes accessed | tf_op | source)
XLA Modules:
  0.0 520.0 jit_solution(9959263662346330774)
XLA Ops:
  7.2 2.7 pad_maximum_fusion
  9.9 11.5 %all-to-all-start = ((bf16[2,32,16,768]{3,2,0,1:T(8,128)(2,1)}), bf16[2,32,16,768]{3,2,0,1:T(8,128)(2,1)S(1)}, u32[]{:S(2)}, u32[]{:S(2)}) async-start(bf16[2,32,16,768]{3,2,0,1:T(8,128)(2,1)} %pad_maximum_fusion), calls=%async_computation | async-start | bytes 3145728 | tf_op jit(solution)/shard_map/all_to_all | solution.py:90
  21.3 2.2 multiply_convert_fusion.7
  23.6 36.9 %all-to-all-done = bf16[2,32,16,768]{3,2,0,1:T(8,128)(2,1)S(1)} async-done(((bf16[2,32,16,768]{3,2,0,1:T(8,128)(2,1)}), bf16[2,32,16,768]{3,2,0,1:T(8,128)(2,1)S(1)}, u32[]{:S(2)}, u32[]{:S(2)}) %all-to-all-start) | async-done | bytes 1572896 | tf_op jit(solution)/shard_map/all_to_all | solution.py:90
  60.6 1.0 convolution_bitcast_fusion.2
  62.1 1.9 copy.79
  64.0 25.0 %all_to_all.84 = bf16[2,1,2,256,768]{4,0,2,1,3:T(2,128)(2,1)S(1)} all-to-all(bf16[2,1,2,256,768]{4,0,2,1,3:T(2,128)(2,1)S(1)} %copy.79), channel_id=1, replica_groups=mesh['lat'=8,'lon'=32] {'lat'}, dimensions={3} | all-to-all | bytes 3145728 | tf_op jit(solution)/shard_map/all_to_all | solution.py:120
  89.2 2.0 copy.81
  91.2 5.9 %all-to-all-start.2 = ((bf16[2,8,2,32,768]{4,1,2,0,3:T(8,128)(2,1)}), bf16[2,8,2,32,768]{4,1,2,0,3:T(8,128)(2,1)S(1)}, u32[]{:S(2)}, u32[]{:S(2)}) async-start(bf16[2,8,2,32,768]{4,1,2,0,3:T(8,128)(2,1)} %copy.81), calls=%async_computation.2 | async-start | bytes 3145728 | tf_op jit(solution)/shard_map/all_to_all | solution.py:119
  97.2 1.1 multiply_convert_fusion.9
  98.3 1.1 multiply_convert_fusion.12
  99.5 36.3 %all-to-all-done.2 = bf16[2,8,2,32,768]{4,1,2,0,3:T(8,128)(2,1)S(1)} async-done(((bf16[2,8,2,32,768]{4,1,2,0,3:T(8,128)(2,1)}), bf16[2,8,2,32,768]{4,1,2,0,3:T(8,128)(2,1)S(1)}, u32[]{:S(2)}, u32[]{:S(2)}) %all-to-all-start.2) | async-done | bytes 1572896 | tf_op jit(solution)/shard_map/all_to_all | solution.py:119
  135.7 1.0 convolution_bitcast_fusion.1
  136.8 0.4 fusion.4
  137.2 0.6 copy-done.2
  138.1 0.3 fusion.96
  138.5 0.5 multiply_convert_fusion.4
  138.9 0.5 copy-done.7
  139.7 0.3 fusion.76
  140.2 0.5 multiply_convert_fusion.3
  140.7 0.4 subtract_convert_fusion.1
  141.4 0.4 subtract_convert_fusion
  142.1 0.6 fusion.27
  142.9 0.6 fusion.28
  144.3 1.0 convolution_bitcast_fusion
  145.9 3.1 copy.98
  149.0 25.3 %all_to_all.85 = bf16[2,256,2,1,768]{4,0,3,2,1:T(2,128)(2,1)S(1)} all-to-all(bf16[2,256,2,1,768]{4,0,3,2,1:T(2,128)(2,1)} %copy.98), channel_id=1, replica_groups=mesh['lat'=8,'lon'=32] {'lat'}, dimensions={1} | all-to-all | bytes 3145728 | tf_op jit(solution)/shard_map/all_to_all | solution.py:174
  174.5 2.0 copy.100
  176.6 6.0 %all-to-all-start.4 = ((bf16[2,32,2,8,768]{4,3,2,0,1:T(8,128)(2,1)}), bf16[2,32,2,8,768]{4,3,2,0,1:T(8,128)(2,1)S(1)}, u32[]{:S(2)}, u32[]{:S(2)}) async-start(bf16[2,32,2,8,768]{4,3,2,0,1:T(8,128)(2,1)} %copy.100), calls=%async_computation.4 | async-start | bytes 3145728 | tf_op jit(solution)/shard_map/all_to_all | solution.py:173
  182.6 3.2 multiply_convert_fusion.6
  185.8 35.3 %all-to-all-done.4 = bf16[2,32,2,8,768]{4,3,2,0,1:T(8,128)(2,1)S(1)} async-done(((bf16[2,32,2,8,768]{4,3,2,0,1:T(8,128)(2,1)}), bf16[2,32,2,8,768]{4,3,2,0,1:T(8,128)(2,1)S(1)}, u32[]{:S(2)}, u32[]{:S(2)}) %all-to-all-start.4) | async-done | bytes 1572896 | tf_op jit(solution)/shard_map/all_to_all | solution.py:173
  221.3 0.8 copy-done.11
  222.2 0.6 fusion.18
  222.8 0.7 fusion.17
  223.7 3.0 copy.102
  226.6 5.8 %all-to-all-start.5 = ((bf16[2,1,512,768]{3,0,1,2:T(2,128)(2,1)}), bf16[2,1,512,768]{3,0,1,2:T(2,128)(2,1)S(1)}, u32[]{:S(2)}, u32[]{:S(2)}) async-start(bf16[2,1,512,768]{3,0,1,2:T(2,128)(2,1)} %copy.102), calls=%async_computation.5 | async-start | bytes 3145728 | tf_op jit(solution)/shard_map/all_to_all | solution.py:90
  232.5 1.3 fusion.127
  233.8 1.3 fusion.32
  235.7 0.9 pad_maximum_fusion.5
  237.7 0.9 pad_maximum_fusion.4
  238.6 264.8 %all-reduce.3.cloned.1.call-done = (f32[2,8,96,96]{3,2,1,0:T(8,128)}, f32[2,8,96,96]{3,2,1,0:T(8,128)}) async-done(((f32[2,8,96,96]{3,2,1,0:T(8,128)}, f32[2,8,96,96]{3,2,1,0:T(8,128)}), (f32[2,8,96,96]{3,2,1,0:T(8,128)}, f32[2,8,96,96]{3,2,1,0:T(8,128)})) %all-reduce.3.cloned.1.call-update) | async-done | bytes 1179664 | tf_op jit(solution)/shard_map/psum | solution.py:204
  503.4 2.2 broadcast_multiply_fusion
  505.6 0.9 broadcast_multiply_fusion.1
  506.5 2.2 fusion.123
  508.9 1.0 copy-done.8
  509.9 1.1 fusion.13
  511.1 1.0 copy-done.9
  512.1 1.1 fusion.14
  (59 shorter events, 6.1 us)
Async XLA Ops:
  9.9 50.6 %all-to-all-start = ((bf16[2,32,16,768]{3,2,0,1:T(8,128)(2,1)}), bf16[2,32,16,768]{3,2,0,1:T(8,128)(2,1)S(1)}, u32[]{:S(2)}, u32[]{:S(2)}) async-start(bf16[2,32,16,768]{3,2,0,1:T(8,128)(2,1)} %pad_maximum_fusion), calls=%async_computation | async-start | bytes 3145728 | tf_op jit(solution)/shard_map/all_to_all | solution.py:90
  91.2 44.5 %all-to-all-start.2 = ((bf16[2,8,2,32,768]{4,1,2,0,3:T(8,128)(2,1)}), bf16[2,8,2,32,768]{4,1,2,0,3:T(8,128)(2,1)S(1)}, u32[]{:S(2)}, u32[]{:S(2)}) async-start(bf16[2,8,2,32,768]{4,1,2,0,3:T(8,128)(2,1)} %copy.81), calls=%async_computation.2 | async-start | bytes 3145728 | tf_op jit(solution)/shard_map/all_to_all | solution.py:119
  136.8 1.0 copy-start.2
  138.4 1.0 copy-start.7
  141.1 1.8 copy-start.3
  141.8 0.9 copy-start.5
  143.5 0.8 copy-start
  176.6 44.5 %all-to-all-start.4 = ((bf16[2,32,2,8,768]{4,3,2,0,1:T(8,128)(2,1)}), bf16[2,32,2,8,768]{4,3,2,0,1:T(8,128)(2,1)S(1)}, u32[]{:S(2)}, u32[]{:S(2)}) async-start(bf16[2,32,2,8,768]{4,3,2,0,1:T(8,128)(2,1)} %copy.100), calls=%async_computation.4 | async-start | bytes 3145728 | tf_op jit(solution)/shard_map/all_to_all | solution.py:173
  221.2 1.0 copy-start.11
  221.2 1.0 copy-start.12
  226.6 279.9 %all-to-all-start.5 = ((bf16[2,1,512,768]{3,0,1,2:T(2,128)(2,1)}), bf16[2,1,512,768]{3,0,1,2:T(2,128)(2,1)S(1)}, u32[]{:S(2)}, u32[]{:S(2)}) async-start(bf16[2,1,512,768]{3,0,1,2:T(2,128)(2,1)} %copy.102), calls=%async_computation.5 | async-start | bytes 3145728 | tf_op jit(solution)/shard_map/all_to_all | solution.py:90
  232.4 271.0 %all-reduce.3.cloned.1.call-start = ((), (), s32[]{:S(2)}) async-start(), calls=%async_computation.6 | async-start | bytes 3145728 | tf_op jit(solution)/shard_map/psum | solution.py:204
  232.5 2.6 copy-start.6
  233.8 1.6 copy-start.4
  235.7 1.2 copy-start.1
  503.4 2.2 copy-start.10
  508.8 1.1 copy-start.8
  511.0 1.1 copy-start.9
Sparse Core Ops, SparseCore 0:
  239.4 263.9 all-reduce.2
where the time goes:
time: 521 us; the launch traced here: 520 us
  waiting for transfers between devices  373 us (72%)
  blocking collectives  50.3 us (10%)
  starting transfers between devices  29.2 us (6%)
  local copies, waits for them, and re-layouts  19.4 us (4%)
  other arithmetic  19 us (4%)
  between operations  14.6 us (3%)
  matrix products  14.2 us (3%)
    psum x1, waiting for transfers between devices, shards(): summed = lax.psum((grad_first, grad_second), ('lat', 'lon'))  265 us
    all_to_all x2, waiting for transfers between devices, lon_transpose(): lax.all_to_all(source, 'lon', split_axis=split_dim, concat_axis=concat_di...  36.9 us
    all_to_all x1, waiting for transfers between devices, shards(): lax.all_to_all(lax.all_to_all(spectral_rows, 'lat', split_axis=3, concat_...  36.3 us
    all_to_all x1, waiting for transfers between devices, shards(): lax.all_to_all(lax.all_to_all(inverse_rows, 'lat', split_axis=1, concat_a...  35.3 us
    all_to_all x1, blocking collectives, shards(): lax.all_to_all(inverse_rows, 'lat', split_axis=1, concat_axis=3, tiled=True)  25.3 us
    all_to_all x1, blocking collectives, shards(): lax.all_to_all(spectral_rows, 'lat', split_axis=3, concat_axis=1, tiled=T...  25 us
    all_to_all x2, starting transfers between devices, lon_transpose(): lax.all_to_all(source, 'lon', split_axis=split_dim, concat_axis=concat_di...  17.3 us
  transfers between devices with their start and end apart: 5, of which 4 were waited for; matrix products, arithmetic and copies ran while one was open for 3% of the time, Pallas kernels for 0%

commit v1 on v0

--- a/solution.py
+++ b/solution.py
@@ -201,7 +201,7 @@
     feature_grad = (cotangent.astype(jnp.float32) + spatial[1].astype(jnp.float32)).astype(
         jnp.bfloat16
     )
-    summed = lax.psum((grad_first, grad_second), ("lat", "lon"))
+    summed = lax.psum(lax.psum((grad_first, grad_second), "lat"), "lon")
     factor = 1.0 / math.sqrt(rows_total * kept_total)
     return (mixed_field, feature_grad, summed[0] * factor, summed[1] * factor)
 

time: 521 us -> 479 us (0.919)
  waiting for transfers between devices: 373 us -> 329 us
    psum x1 -> x2, waiting for transfers between devices: 265 us -> 225 us  [shards(): summed = lax.psum(lax.psum((grad_first, grad_second), 'lat'), 'lon')]
  transfers between devices with their start and end apart: 5 -> 6, of which waited for: 4 -> 5; matrix products, arithmetic and copies ran while one was open for 3% -> 4% of each run, Pallas kernels for 0% -> 0%
where the time goes in v1:
time: 479 us; the launch traced here: 478 us
  waiting for transfers between devices  329 us (69%)
  blocking collectives  50.3 us (11%)
  starting transfers between devices  29.4 us (6%)
  other arithmetic  20.1 us (4%)
  local copies, waits for them, and re-layouts  19.5 us (4%)
  matrix products  15.4 us (3%)
  between operations  14.6 us (3%)
    psum x2, waiting for transfers between devices, shards(): summed = lax.psum(lax.psum((grad_first, grad_second), 'lat'), 'lon')  225 us
    all_to_all x2, waiting for transfers between devices, lon_transpose(): lax.all_to_all(source, 'lon', split_axis=split_dim, concat_axis=concat_di...  36.9 us
    all_to_all x1, waiting for transfers between devices, shards(): lax.all_to_all(lax.all_to_all(spectral_rows, 'lat', split_axis=3, concat_...  36.3 us
    all_to_all x1, waiting for transfers between devices, shards(): lax.all_to_all(lax.all_to_all(inverse_rows, 'lat', split_axis=1, concat_a...  30.7 us
    all_to_all x1, blocking collectives, shards(): lax.all_to_all(inverse_rows, 'lat', split_axis=1, concat_axis=3, tiled=True)  25.3 us
    all_to_all x1, blocking collectives, shards(): lax.all_to_all(spectral_rows, 'lat', split_axis=3, concat_axis=1, tiled=T...  25 us
    all_to_all x2, starting transfers between devices, lon_transpose(): lax.all_to_all(source, 'lon', split_axis=split_dim, concat_axis=concat_di...  17.4 us
  transfers between devices with their start and end apart: 6, of which 5 were waited for; matrix products, arithmetic and copies ran while one was open for 4% of the time, Pallas kernels for 0%

profile of v1, /device:TPU:2, one launch (start us, length us, event | category | flops | bytes accessed | tf_op | source)
XLA Modules:
  0.0 477.8 jit_solution(3756489223663425037)
XLA Ops:
  7.2 2.7 pad_maximum_fusion
  9.9 11.5 %all-to-all-start = ((bf16[2,32,16,768]{3,2,0,1:T(8,128)(2,1)}), bf16[2,32,16,768]{3,2,0,1:T(8,128)(2,1)S(1)}, u32[]{:S(2)}, u32[]{:S(2)}) async-start(bf16[2,32,16,768]{3,2,0,1:T(8,128)(2,1)} %pad_maximum_fusion), calls=%async_computation | async-start | bytes 3145728 | tf_op jit(solution)/shard_map/all_to_all | solution.py:90
  21.4 2.2 multiply_convert_fusion.7
  23.6 36.9 %all-to-all-done = bf16[2,32,16,768]{3,2,0,1:T(8,128)(2,1)S(1)} async-done(((bf16[2,32,16,768]{3,2,0,1:T(8,128)(2,1)}), bf16[2,32,16,768]{3,2,0,1:T(8,128)(2,1)S(1)}, u32[]{:S(2)}, u32[]{:S(2)}) %all-to-all-start) | async-done | bytes 1572896 | tf_op jit(solution)/shard_map/all_to_all | solution.py:90
  60.6 1.0 convolution_bitcast_fusion.2
  62.1 1.9 copy.79
  64.0 25.0 %all_to_all.84 = bf16[2,1,2,256,768]{4,0,2,1,3:T(2,128)(2,1)S(1)} all-to-all(bf16[2,1,2,256,768]{4,0,2,1,3:T(2,128)(2,1)S(1)} %copy.79), channel_id=1, replica_groups=mesh['lat'=8,'lon'=32] {'lat'}, dimensions={3} | all-to-all | bytes 3145728 | tf_op jit(solution)/shard_map/all_to_all | solution.py:120
  89.2 2.1 copy.81
  91.3 5.9 %all-to-all-start.2 = ((bf16[2,8,2,32,768]{4,1,2,0,3:T(8,128)(2,1)}), bf16[2,8,2,32,768]{4,1,2,0,3:T(8,128)(2,1)S(1)}, u32[]{:S(2)}, u32[]{:S(2)}) async-start(bf16[2,8,2,32,768]{4,1,2,0,3:T(8,128)(2,1)} %copy.81), calls=%async_computation.2 | async-start | bytes 3145728 | tf_op jit(solution)/shard_map/all_to_all | solution.py:119
  97.2 1.1 multiply_convert_fusion.9
  98.4 1.1 multiply_convert_fusion.12
  99.5 36.3 %all-to-all-done.2 = bf16[2,8,2,32,768]{4,1,2,0,3:T(8,128)(2,1)S(1)} async-done(((bf16[2,8,2,32,768]{4,1,2,0,3:T(8,128)(2,1)}), bf16[2,8,2,32,768]{4,1,2,0,3:T(8,128)(2,1)S(1)}, u32[]{:S(2)}, u32[]{:S(2)}) %all-to-all-start.2) | async-done | bytes 1572896 | tf_op jit(solution)/shard_map/all_to_all | solution.py:119
  135.8 1.0 convolution_bitcast_fusion.1
  137.3 0.6 copy-done.2
  138.5 0.5 multiply_convert_fusion.4
  139.0 0.5 copy-done.7
  140.2 0.5 multiply_convert_fusion.3
  140.7 0.4 subtract_convert_fusion.1
  141.4 0.4 subtract_convert_fusion
  142.1 0.6 fusion.27
  143.0 0.6 fusion.28
  144.4 1.0 convolution_bitcast_fusion
  145.9 3.1 copy.98
  149.1 25.3 %all_to_all.85 = bf16[2,256,2,1,768]{4,0,3,2,1:T(2,128)(2,1)S(1)} all-to-all(bf16[2,256,2,1,768]{4,0,3,2,1:T(2,128)(2,1)} %copy.98), channel_id=1, replica_groups=mesh['lat'=8,'lon'=32] {'lat'}, dimensions={1} | all-to-all | bytes 3145728 | tf_op jit(solution)/shard_map/all_to_all | solution.py:174
  174.6 2.1 copy.100
  176.6 6.0 %all-to-all-start.4 = ((bf16[2,32,2,8,768]{4,3,2,0,1:T(8,128)(2,1)}), bf16[2,32,2,8,768]{4,3,2,0,1:T(8,128)(2,1)S(1)}, u32[]{:S(2)}, u32[]{:S(2)}) async-start(bf16[2,32,2,8,768]{4,3,2,0,1:T(8,128)(2,1)} %copy.100), calls=%async_computation.4 | async-start | bytes 3145728 | tf_op jit(solution)/shard_map/all_to_all | solution.py:173
  182.7 3.2 multiply_convert_fusion.6
  185.9 1.2 fusion.127
  187.2 1.0 fusion.32
  188.4 1.0 fusion.31
  189.5 1.0 fusion.125
  190.5 30.7 %all-to-all-done.4 = bf16[2,32,2,8,768]{4,3,2,0,1:T(8,128)(2,1)S(1)} async-done(((bf16[2,32,2,8,768]{4,3,2,0,1:T(8,128)(2,1)}), bf16[2,32,2,8,768]{4,3,2,0,1:T(8,128)(2,1)S(1)}, u32[]{:S(2)}, u32[]{:S(2)}) %all-to-all-start.4) | async-done | bytes 1572896 | tf_op jit(solution)/shard_map/all_to_all | solution.py:173
  221.4 0.8 copy-done.13
  222.3 0.6 fusion.18
  222.9 0.7 fusion.17
  223.7 3.0 copy.102
  226.7 5.9 %all-to-all-start.5 = ((bf16[2,1,512,768]{3,0,1,2:T(2,128)(2,1)}), bf16[2,1,512,768]{3,0,1,2:T(2,128)(2,1)S(1)}, u32[]{:S(2)}, u32[]{:S(2)}) async-start(bf16[2,1,512,768]{3,0,1,2:T(2,128)(2,1)} %copy.102), calls=%async_computation.5 | async-start | bytes 3145728 | tf_op jit(solution)/shard_map/all_to_all | solution.py:90
  232.7 2.0 pad_maximum_fusion.5
  235.5 0.9 pad_maximum_fusion.4
  236.5 67.8 %all-reduce.7.cloned.1.call-done = (f32[2,8,96,96]{3,2,1,0:T(8,128)}, f32[2,8,96,96]{3,2,1,0:T(8,128)}) async-done(((f32[2,8,96,96]{3,2,1,0:T(8,128)}, f32[2,8,96,96]{3,2,1,0:T(8,128)}), (f32[2,8,96,96]{3,2,1,0:T(8,128)}, f32[2,8,96,96]{3,2,1,0:T(8,128)})) %all-reduce.7.cloned.1.call-update) | async-done | bytes 1179664 | tf_op jit(solution)/shard_map/psum | solution.py:204
  304.3 156.9 %all-reduce.5.cloned.1.call-done = (f32[2,8,96,96]{3,2,1,0:T(8,128)}, f32[2,8,96,96]{3,2,1,0:T(8,128)}) async-done(((f32[2,8,96,96]{3,2,1,0:T(8,128)}, f32[2,8,96,96]{3,2,1,0:T(8,128)}), (f32[2,8,96,96]{3,2,1,0:T(8,128)}, f32[2,8,96,96]{3,2,1,0:T(8,128)})) %all-reduce.5.cloned.1.call-update) | async-done | bytes 1179664 | tf_op jit(solution)/shard_map/psum | solution.py:204
  461.3 2.2 broadcast_multiply_fusion
  463.4 0.9 broadcast_multiply_fusion.1
  464.4 2.2 fusion.123
  466.7 1.0 copy-done.8
  467.7 1.1 fusion.13
  468.9 1.0 copy-done.9
  469.9 1.1 fusion.14
  (66 shorter events, 6.7 us)
Async XLA Ops:
  9.9 50.6 %all-to-all-start = ((bf16[2,32,16,768]{3,2,0,1:T(8,128)(2,1)}), bf16[2,32,16,768]{3,2,0,1:T(8,128)(2,1)S(1)}, u32[]{:S(2)}, u32[]{:S(2)}) async-start(bf16[2,32,16,768]{3,2,0,1:T(8,128)(2,1)} %pad_maximum_fusion), calls=%async_computation | async-start | bytes 3145728 | tf_op jit(solution)/shard_map/all_to_all | solution.py:90
  91.3 44.5 %all-to-all-start.2 = ((bf16[2,8,2,32,768]{4,1,2,0,3:T(8,128)(2,1)}), bf16[2,8,2,32,768]{4,1,2,0,3:T(8,128)(2,1)S(1)}, u32[]{:S(2)}, u32[]{:S(2)}) async-start(bf16[2,8,2,32,768]{4,1,2,0,3:T(8,128)(2,1)} %copy.81), calls=%async_computation.2 | async-start | bytes 3145728 | tf_op jit(solution)/shard_map/all_to_all | solution.py:119
  136.8 1.0 copy-start.2
  138.4 1.0 copy-start.7
  141.1 1.8 copy-start.3
  141.8 0.9 copy-start.5
  143.6 0.8 copy-start
  176.6 44.5 %all-to-all-start.4 = ((bf16[2,32,2,8,768]{4,3,2,0,1:T(8,128)(2,1)}), bf16[2,32,2,8,768]{4,3,2,0,1:T(8,128)(2,1)S(1)}, u32[]{:S(2)}, u32[]{:S(2)}) async-start(bf16[2,32,2,8,768]{4,3,2,0,1:T(8,128)(2,1)} %copy.100), calls=%async_computation.4 | async-start | bytes 3145728 | tf_op jit(solution)/shard_map/all_to_all | solution.py:173
  182.6 4.5 copy-start.6
  187.1 1.3 copy-start.4
  221.3 1.0 copy-start.13
  221.3 1.0 copy-start.14
  226.7 6.0 %copy-start.10 = (f32[1,8,96,96]{3,2,1,0:T(8,128)S(1)}, f32[1,8,96,96]{3,2,1,0:T(8,128)}, u32[]{:S(2)}) copy-start(f32[1,8,96,96]{3,2,1,0:T(8,128)} %fusion.32) | copy-start | bytes 884740
  226.7 237.7 %all-to-all-start.5 = ((bf16[2,1,512,768]{3,0,1,2:T(2,128)(2,1)}), bf16[2,1,512,768]{3,0,1,2:T(2,128)(2,1)S(1)}, u32[]{:S(2)}, u32[]{:S(2)}) async-start(bf16[2,1,512,768]{3,0,1,2:T(2,128)(2,1)} %copy.102), calls=%async_computation.5 | async-start | bytes 3145728 | tf_op jit(solution)/shard_map/all_to_all | solution.py:90
  232.6 2.1 copy-start.1
  232.6 71.7 %all-reduce.7.cloned.1.call-start = ((), (), s32[]{:S(2)}) async-start(), calls=%async_computation.7 | async-start | bytes 3145728 | tf_op jit(solution)/shard_map/psum | solution.py:204
  232.7 2.0 copy-start.11
  236.5 224.8 %all-reduce.5.cloned.1.call-start = ((), (), s32[]{:S(2)}) async-start(), calls=%async_computation.6 | async-start | bytes 3145728 | tf_op jit(solution)/shard_map/psum | solution.py:204
  461.3 2.2 copy-start.12
  466.6 1.1 copy-start.8
  468.8 1.1 copy-start.9
Sparse Core Ops, SparseCore 0:
  236.6 67.6 all-reduce.6
  307.8 153.4 all-reduce.4
